TPU v7x, 512 devices: a whole 4x8x8 slice. The times are simulated.
512 devices in a mesh: dom: 8 (over y_hi, core), fsdp: 64 (over x, z, y_lo).
Axes of the slice: x: 4, y: 8 (y_hi: 4, y_lo: 2; y = y_hi * 2 + y_lo), z: 8, core: 2. Of those that a mesh axis runs over, the one named last changes fastest.
Arguments:
- weights: bfloat16 [8, 64, 640, 896], P('dom', 'fsdp'), may hold values from -6 to 6
- activations: bfloat16 [8, 2, 1280, 2560], P('dom', None, 'fsdp'), may hold values from -6 to 6
- cotangents: bfloat16 [8, 2, 1280, 14336], P('dom', None, 'fsdp'), may hold values from -0.15625 to 0.15625
- lengths: int32 [8, 2, 64], P('dom', None, 'fsdp'), may hold values from 1 to 20, 960 in all within a row
Outputs:
- merged: bfloat16 [64, 640, 896], P('fsdp')
Inputs may be any that keep to these rules, and one draw needn't show every extreme that they name: In every domain and micro-batch the lengths sum to 960, and some block is full.
All inputs are finite; a program needn't handle non-finite values.
Results may differ from a plain program's by a relative error of at most 0.018.
Values may be sent and summed in bfloat16 or wider, within the bound.
No kernel may reach another device: no remote copies, remote signals or barrier semaphores. Data moves between devices by JAX's collectives and lax.ppermute only.
A program may use at most 64 MiB of HBM per device.

v0:
```python
import jax
import jax.numpy as jnp
from jax import lax
from jax.sharding import PartitionSpec as P

damping = 0.001


def squares(pieces):
    feat_rows, cot_rows = pieces
    grad = jnp.einsum("nmsr,nmsc->mrc", feat_rows, cot_rows, preferred_element_type=jnp.float32)
    return grad * grad


def body(weights, activations, cotangents, lengths):
    devices = lax.axis_size("fsdp")
    rows = weights.shape[2]
    cols = weights.shape[3]
    batches = activations.shape[1]
    slots = activations.shape[2]
    row_blocks = activations.shape[3] // rows
    col_blocks = devices // row_blocks
    mask = (jnp.arange(slots)[None, :] < lengths[0, :, 0:1]).astype(jnp.bfloat16)
    feats = activations[0] * mask[:, :, None]
    feat_blocks = feats.reshape(batches, slots, row_blocks, rows).transpose(2, 0, 1, 3)
    feat_send = jnp.broadcast_to(
        feat_blocks[:, None], (row_blocks, col_blocks, batches, slots, rows)
    ).reshape(devices, batches, slots, rows)
    cot_blocks = cotangents[0].reshape(batches, slots, col_blocks, cols).transpose(2, 0, 1, 3)
    cot_send = jnp.broadcast_to(
        cot_blocks[None], (row_blocks, col_blocks, batches, slots, cols)
    ).reshape(devices, batches, slots, cols)
    squared = squares(
        (
            lax.all_to_all(feat_send, "fsdp", split_axis=0, concat_axis=0, tiled=True),
            lax.all_to_all(cot_send, "fsdp", split_axis=0, concat_axis=0, tiled=True),
        )
    )
    fisher = jnp.sum(squared, axis=0) / batches
    term = fisher + damping
    numer_term = term * weights[0, 0].astype(jnp.float32)
    numer, denom = (
        lax.psum(numer_term.astype(jnp.bfloat16), "dom").astype(jnp.float32),
        lax.psum(term.astype(jnp.bfloat16), "dom").astype(jnp.float32),
    )
    merged = (numer / denom).astype(jnp.bfloat16)
    return merged[None]


def solution(mesh):
    return jax.shard_map(
        body,
        mesh=mesh,
        in_specs=(
            P("dom", "fsdp", None, None),
            P("dom", None, "fsdp", None),
            P("dom", None, "fsdp", None),
            P("dom", None, "fsdp"),
        ),
        out_specs=P("fsdp", None, None),
        check_vma=False,
    )
```

profile of v0, /device:TPU:19, one launch (start us, length us, event | category | flops | bytes accessed | tf_op | source)
XLA Modules:
  0.0 328.0 jit_solution(18246231903309940472)
XLA Ops:
  6.5 1.1 squeeze.2
  7.6 0.7 fusion.11
  8.3 0.2 multiply_bitcast_fusion
  8.4 0.2 copy.11
  8.6 3.4 %broadcast_in_dim.6 = bf16[4,16,2,20,640]{4,2,3,1,0:T(2,128)(2,1)} broadcast(bf16[4,2,20,640]{3,1,2,0:T(2,128)(2,1)S(1)} %copy.11), dimensions={0,2,3,4} | broadcast | bytes 3481600 | tf_op jit(solution)/shard_map/broadcast_in_dim | solution.py:26
  12.0 0.0 copy-start
  12.0 14.6 %all-to-all-start = ((bf16[64,2,20,640]{3,1,2,0:T(2,128)(2,1)}), bf16[64,2,20,640]{3,1,2,0:T(2,128)(2,1)}, u32[]{:S(2)}, u32[]{:S(2)}) async-start(bf16[64,2,20,640]{3,1,2,0:T(2,128)(2,1)} %bitcast.2), calls=%async_computation | async-start | bytes 6553600 | tf_op jit(solution)/shard_map/all_to_all | solution.py:35
  26.6 0.0 all-reduce.3.cloned.1.call-start
  26.6 0.0 copy-done
  26.7 0.8 reshape_squeeze.3
  27.4 0.9 copy.12
  28.3 70.1 %all-to-all-done = bf16[64,2,20,640]{3,1,2,0:T(2,128)(2,1)} async-done(((bf16[64,2,20,640]{3,1,2,0:T(2,128)(2,1)}), bf16[64,2,20,640]{3,1,2,0:T(2,128)(2,1)}, u32[]{:S(2)}, u32[]{:S(2)}) %all-to-all-start) | async-done | bytes 3276832 | tf_op jit(solution)/shard_map/all_to_all | solution.py:35
  98.4 4.4 %broadcast_in_dim.7 = bf16[4,16,2,20,896]{4,2,3,1,0:T(2,128)(2,1)} broadcast(bf16[16,2,20,896]{3,1,2,0:T(2,128)(2,1)S(1)} %copy.12), dimensions={1,2,3,4} | broadcast | bytes 5734400 | tf_op jit(solution)/shard_map/broadcast_in_dim | solution.py:30
  102.8 114.7 %all_to_all.10 = bf16[64,2,20,896]{3,1,2,0:T(2,128)(2,1)S(1)} all-to-all(bf16[64,2,20,896]{3,1,2,0:T(2,128)(2,1)} %bitcast.20), channel_id=1, replica_groups=mesh['dom'=8,'fsdp'=64] {'fsdp'}, dimensions={0} | all-to-all | bytes 9175040 | tf_op jit(solution)/shard_map/all_to_all | solution.py:36
  217.5 0.0 copy-start.1
  217.5 5.8 %fusion = f32[640,896]{1,0:T(8,128)S(1)} fusion(bf16[64,2,20,896]{3,1,2,0:T(2,128)(2,1)S(1)} %all_to_all.10, bf16[64,2,20,640]{3,1,2,0:T(2,128)(2,1)} %all-to-all-done), kind=kOutput, calls=%fused_computation.1 | convolution fusion | flops 2937733120 | bytes 10158080 | tf_op jit(solution)/shard_map/nmsr,nmsc->mrc/dot_general | solution.py:11
  223.4 0.0 copy-done.1
  223.4 1.8 fusion.4
  225.1 0.0 all-reduce.3.cloned.1.call-update
  225.2 93.0 %all-reduce.3.cloned.1.call-done = (bf16[640,896]{1,0:T(8,128)(2,1)}, bf16[640,896]{1,0:T(8,128)(2,1)}) async-done(((bf16[640,896]{1,0:T(8,128)(2,1)}, bf16[640,896]{1,0:T(8,128)(2,1)}), (bf16[640,896]{1,0:T(8,128)(2,1)}, bf16[640,896]{1,0:T(8,128)(2,1)})) %all-reduce.3.cloned.1.call-update) | async-done | bytes 2293776 | tf_op jit(solution)/shard_map/psum | solution.py:44
  318.2 3.0 fusion.10
Async XLA Ops:
  12.0 14.7 %copy-start = (bf16[1,2,20,14336]{3,1,2,0:T(2,128)(2,1)S(1)}, bf16[1,2,20,14336]{3,1,2,0:T(2,128)(2,1)}, u32[]{:S(2)}) copy-start(bf16[1,2,20,14336]{3,1,2,0:T(2,128)(2,1)} %param.6) | copy-start | bytes 3440644
  12.0 86.5 %all-to-all-start = ((bf16[64,2,20,640]{3,1,2,0:T(2,128)(2,1)}), bf16[64,2,20,640]{3,1,2,0:T(2,128)(2,1)}, u32[]{:S(2)}, u32[]{:S(2)}) async-start(bf16[64,2,20,640]{3,1,2,0:T(2,128)(2,1)} %bitcast.2), calls=%async_computation | async-start | bytes 6553600 | tf_op jit(solution)/shard_map/all_to_all | solution.py:35
  26.6 291.6 %all-reduce.3.cloned.1.call-start = ((), (), s32[]{:S(2)}) async-start(), calls=%async_computation.2 | async-start | bytes 4587520 | tf_op jit(solution)/shard_map/psum | solution.py:44
  217.5 5.8 %copy-start.1 = (bf16[1,1,640,896]{3,2,1,0:T(8,128)(2,1)S(1)}, bf16[1,1,640,896]{3,2,1,0:T(8,128)(2,1)}, u32[]{:S(2)}) copy-start(bf16[1,1,640,896]{3,2,1,0:T(8,128)(2,1)} %param.4) | copy-start | bytes 3440644
Sparse Core Ops, SparseCore 0:
  225.3 92.8 all-reduce.2
where the time goes:
time: 328 us
  waiting for transfers between devices  163 us (50%)
  blocking collectives  115 us (35%)
  starting transfers between devices  14.7 us (4%)
  between operations  13.5 us (4%)
  local copies, waits for them, and re-layouts  10.7 us (3%)
  matrix products  5.84 us (2%)
  other arithmetic  5.63 us (2%)
    all_to_all x1, blocking collectives, body(): lax.all_to_all(cot_send, 'fsdp', split_axis=0, concat_axis=0, tiled=True)  115 us
    psum x1, waiting for transfers between devices, body(): lax.psum(term.astype(jnp.bfloat16), 'dom').astype(jnp.float32)  93 us
    all_to_all x1, waiting for transfers between devices, body(): lax.all_to_all(feat_send, 'fsdp', split_axis=0, concat_axis=0, tiled=True)  70.1 us
    all_to_all x1, starting transfers between devices, body(): lax.all_to_all(feat_send, 'fsdp', split_axis=0, concat_axis=0, tiled=True)  14.6 us
  transfers between devices with their start and end apart: 2, of which 2 were waited for; matrix products, arithmetic and copies ran while one was open for 1% of the time, Pallas kernels for 0%

commit v1 on v0

--- a/solution.py
+++ b/solution.py
@@ -41,7 +41,7 @@
     numer_term = term * weights[0, 0].astype(jnp.float32)
     numer, denom = (
         lax.psum(numer_term.astype(jnp.bfloat16), "dom").astype(jnp.float32),
-        lax.psum(term.astype(jnp.bfloat16), "dom").astype(jnp.float32),
+        jnp.sum(lax.all_gather(term.astype(jnp.bfloat16), "dom"), axis=0).astype(jnp.float32),
     )
     merged = (numer / denom).astype(jnp.bfloat16)
     return merged[None]

time: 328 us -> 417 us (1.27)
  the two profiles are of different devices: /device:TPU:19 before, /device:TPU:17 now
where the time goes in v1:
time: 417 us; the launch traced here: 416 us
  waiting for transfers between devices  248 us (59%)
  blocking collectives  112 us (27%)
  starting transfers between devices  15 us (4%)
  between operations  13.5 us (3%)
  other arithmetic  10.9 us (3%)
  local copies, waits for them, and re-layouts  10.7 us (3%)
  matrix products  5.84 us (1%)
    all_to_all x1, blocking collectives, body(): lax.all_to_all(cot_send, 'fsdp', split_axis=0, concat_axis=0, tiled=True)  112 us
    all_gather x1, waiting for transfers between devices, body(): lax.all_gather(term.astype(jnp.bfloat16), 'dom')  94.9 us
    psum x1, waiting for transfers between devices, body(): lax.psum(numer_term.astype(jnp.bfloat16), 'dom').astype(jnp.float32)  80.4 us
    all_to_all x1, waiting for transfers between devices, body(): lax.all_to_all(feat_send, 'fsdp', split_axis=0, concat_axis=0, tiled=True)  72.4 us
    all_to_all x1, starting transfers between devices, body(): lax.all_to_all(feat_send, 'fsdp', split_axis=0, concat_axis=0, tiled=True)  14.9 us
  transfers between devices with their start and end apart: 3, of which 3 were waited for; matrix products, arithmetic and copies ran while one was open for 2% of the time, Pallas kernels for 0%

profile of v1, /device:TPU:17, one launch (start us, length us, event | category | flops | bytes accessed | tf_op | source)
XLA Modules:
  0.0 416.3 jit_solution(13682991294371484641)
XLA Ops:
  6.5 1.1 squeeze.2
  7.6 0.7 fusion.11
  8.3 0.2 multiply_bitcast_fusion
  8.4 0.2 copy.11
  8.6 3.4 broadcast_in_dim.6
  12.0 0.0 copy-start
  12.0 14.9 %all-to-all-start = ((bf16[64,2,20,640]{3,1,2,0:T(2,128)(2,1)}), bf16[64,2,20,640]{3,1,2,0:T(2,128)(2,1)}, u32[]{:S(2)}, u32[]{:S(2)}) async-start(bf16[64,2,20,640]{3,1,2,0:T(2,128)(2,1)} %bitcast.2), calls=%async_computation | async-start | bytes 6553600 | tf_op jit(solution)/shard_map/all_to_all | solution.py:35
  26.9 0.0 all-gather.3.cloned.1.call-start
  26.9 0.0 copy-done
  26.9 0.8 reshape_squeeze.3
  27.7 0.9 copy.12
  28.6 72.4 %all-to-all-done = bf16[64,2,20,640]{3,1,2,0:T(2,128)(2,1)} async-done(((bf16[64,2,20,640]{3,1,2,0:T(2,128)(2,1)}), bf16[64,2,20,640]{3,1,2,0:T(2,128)(2,1)}, u32[]{:S(2)}, u32[]{:S(2)}) %all-to-all-start) | async-done | bytes 3276832 | tf_op jit(solution)/shard_map/all_to_all | solution.py:35
  101.0 4.4 %broadcast_in_dim.7 = bf16[4,16,2,20,896]{4,2,3,1,0:T(2,128)(2,1)} broadcast(bf16[16,2,20,896]{3,1,2,0:T(2,128)(2,1)S(1)} %copy.12), dimensions={1,2,3,4} | broadcast | bytes 5734400 | tf_op jit(solution)/shard_map/broadcast_in_dim | solution.py:30
  105.4 112.1 %all_to_all.10 = bf16[64,2,20,896]{3,1,2,0:T(2,128)(2,1)S(1)} all-to-all(bf16[64,2,20,896]{3,1,2,0:T(2,128)(2,1)} %bitcast.21), channel_id=1, replica_groups=mesh['dom'=8,'fsdp'=64] {'fsdp'}, dimensions={0} | all-to-all | bytes 9175040 | tf_op jit(solution)/shard_map/all_to_all | solution.py:36
  217.5 5.8 %fusion = f32[640,896]{1,0:T(8,128)S(1)} fusion(bf16[64,2,20,896]{3,1,2,0:T(2,128)(2,1)S(1)} %all_to_all.10, bf16[64,2,20,640]{3,1,2,0:T(2,128)(2,1)} %all-to-all-done), kind=kOutput, calls=%fused_computation.1 | convolution fusion | flops 2937733120 | bytes 10158080 | tf_op jit(solution)/shard_map/nmsr,nmsc->mrc/dot_general | solution.py:11
  223.3 0.0 copy-done.1
  223.4 1.8 fusion.4
  225.1 0.0 all-gather.3.cloned.1.call-update
  225.2 0.0 all-reduce.2.cloned.1.call-start
  225.2 0.7 all-reduce.2.cloned.1.call-update
  225.9 94.9 %all-gather.3.cloned.1.call-done = bf16[5120,896]{1,0:T(8,128)(2,1)} async-done(((bf16[640,896]{1,0:T(8,128)(2,1)}), bf16[5120,896]{1,0:T(8,128)(2,1)}) %all-gather.3.cloned.1.call-update) | async-done | bytes 9175056 | tf_op jit(solution)/shard_map/all_gather | solution.py:44
  320.8 5.6 %reduce_sum.22 = bf16[640,896]{1,0:T(8,128)(2,1)S(1)} reduce(bf16[8,640,896]{2,1,0:T(8,128)(2,1)} %bitcast.22, bf16[]{:T(256)} %constant.8.clone.1), dimensions={0}, to_apply=%region_2.0 | reduce | flops 4014080 | bytes 10321922 | tf_op jit(solution)/shard_map/reduce_sum | solution.py:44
  326.4 80.4 %all-reduce.2.cloned.1.call-done = bf16[640,896]{1,0:T(8,128)(2,1)} async-done(((bf16[640,896]{1,0:T(8,128)(2,1)}), bf16[640,896]{1,0:T(8,128)(2,1)}) %all-reduce.2.cloned.1.call-update) | async-done | bytes 1146896 | tf_op jit(solution)/shard_map/psum | solution.py:43
  406.8 2.7 fusion.10
  (1 shorter events, 0.0 us)
Async XLA Ops:
  12.0 14.9 %copy-start = (bf16[1,2,20,14336]{3,1,2,0:T(2,128)(2,1)S(1)}, bf16[1,2,20,14336]{3,1,2,0:T(2,128)(2,1)}, u32[]{:S(2)}) copy-start(bf16[1,2,20,14336]{3,1,2,0:T(2,128)(2,1)} %param.6) | copy-start | bytes 3440644
  12.0 89.0 %all-to-all-start = ((bf16[64,2,20,640]{3,1,2,0:T(2,128)(2,1)}), bf16[64,2,20,640]{3,1,2,0:T(2,128)(2,1)}, u32[]{:S(2)}, u32[]{:S(2)}) async-start(bf16[64,2,20,640]{3,1,2,0:T(2,128)(2,1)} %bitcast.2), calls=%async_computation | async-start | bytes 6553600 | tf_op jit(solution)/shard_map/all_to_all | solution.py:35
  26.9 293.9 %all-gather.3.cloned.1.call-start = ((), (), s32[]{:S(2)}) async-start(), calls=%async_computation.3 | async-start | bytes 10321920 | tf_op jit(solution)/shard_map/all_gather | solution.py:44
  217.5 5.9 %copy-start.1 = (bf16[1,1,640,896]{3,2,1,0:T(8,128)(2,1)S(1)}, bf16[1,1,640,896]{3,2,1,0:T(8,128)(2,1)}, u32[]{:S(2)}) copy-start(bf16[1,1,640,896]{3,2,1,0:T(8,128)(2,1)} %param.4) | copy-start | bytes 3440644
  225.2 181.6 %all-reduce.2.cloned.1.call-start = ((), (), s32[]{:S(2)}) async-start(), calls=%async_computation.2 | async-start | bytes 2293760 | tf_op jit(solution)/shard_map/psum | solution.py:43
Sparse Core Ops, SparseCore 0:
  225.3 95.4 all-gather.2
  323.7 83.0 all-reduce.1
